TPU v7x, 32 devices: a whole 2x2x4 slice. The times are simulated.
32 devices in a mesh: sensor: 2 (over y), tm: 16 (over z, x, core).
Axes of the slice: x: 2, y: 2, z: 4, core: 2. Of those that a mesh axis runs over, the one named last changes fastest.
Arguments:
- recording: bfloat16 [256, 16384], P('sensor', 'tm'), may hold values from -6 to 6
- spatial_w: bfloat16 [512, 256], P(None, 'sensor'), may hold values from -0.375 to 0.375
- conv_w: bfloat16 [3, 3, 512, 512], P(None, None, 'sensor'), may hold values from -0.15625 to 0.15625
- conv_b: float32 [3, 512], P(None, 'sensor'), may hold values from -3 to 3
- dilations: int32 [3], replicated, may hold values from 1 to 16, as said below
- valid_frames: int32 [16], P('tm'), may hold values from 512 to 1024, as said below
- key_w: bfloat16 [512, 512], P('sensor'), may hold values from -0.25 to 0.25
- value_w: bfloat16 [512, 512], P('sensor'), may hold values from -0.25 to 0.25
- queries: bfloat16 [512, 2048], P('sensor'), may hold values from -60 to 60
Outputs:
- features: bfloat16 [512, 16384], P('sensor', 'tm')
- attended: bfloat16 [512, 2048], P('sensor')
Inputs may be any that keep to these rules, and one draw needn't show every extreme that they name: `dilations`: one layer has dilation exactly 16 and another exactly 1. `valid_frames`: one block is full and one holds exactly half of its 1024 frames.
All inputs are finite; a program needn't handle non-finite values.
Results may differ from a plain program's by a relative error of at most 0.015.
The roundings to bfloat16 on the way count: a program that leaves them out, or rounds other values in their place, can miss the bound.
Values may be sent and summed in bfloat16 or wider, within the bound.
No kernel may reach another device: no remote copies, remote signals or barrier semaphores. Data moves between devices by JAX's collectives and lax.ppermute only.
A program may use at most 64 MiB of HBM per device.

v0:
```python
import math
import jax
import jax.numpy as jnp
from jax import lax
from jax.sharding import PartitionSpec as P

HD = 64
LATENTS = 2048
LAYERS = 3
DMAX = 16


def padded(cells, sides, width):
    for axis, dim in sides:
        count = lax.axis_size(axis)
        ends = count - 1
        head = lax.slice_in_dim(cells, 0, width, axis=dim)
        tail = lax.slice_in_dim(cells, cells.shape[dim] - width, cells.shape[dim], axis=dim)
        cells = jnp.concatenate(
            [
                lax.ppermute(tail, axis, [(i, (i + 1) % count) for i in range(ends)]),
                cells,
                lax.ppermute(head, axis, [((i + 1) % count, i) for i in range(ends)]),
            ],
            axis=dim,
        )
    return cells


def tap_folder(kernels, dilation, frames, margin):

    def add_taps(running, portion, first_row):
        portion = jnp.pad(portion, ((0, 0), (margin, margin)))
        for tap_index in range(3):
            kernel = kernels[tap_index]
            offset = DMAX + (tap_index - 1) * dilation
            shifted = lax.dynamic_slice_in_dim(portion, offset, frames, 1)
            running = running + jnp.dot(kernel, shifted, preferred_element_type=jnp.float32)
        return running

    return add_taps


def on_device(
    recording, spatial_w, conv_w, conv_b, dilations, valid_frames, key_w, value_w, queries
):
    frames = recording.shape[1]
    ch_loc = conv_w.shape[2]
    hidden = lax.psum_scatter(
        jnp.dot(spatial_w, recording, preferred_element_type=jnp.float32),
        "sensor",
        scatter_dimension=0,
        tiled=True,
    ).astype(jnp.bfloat16)
    reach = 3 * DMAX
    extended = padded(hidden, (("tm", 1),), reach)
    span = frames + 2 * reach
    position = lax.axis_index("tm") * frames - reach + jnp.arange(span, dtype=jnp.int32)
    inside = (position >= 0) & (position < frames * lax.axis_size("tm"))
    for layer in range(LAYERS):
        initial = jnp.broadcast_to(conv_b[layer][:, None], (ch_loc, span))
        folder = tap_folder(conv_w[layer], dilations[layer], span, DMAX)
        preact = folder(
            initial, lax.all_gather(extended, "sensor", axis=0, tiled=True), jnp.int32(0)
        )
        updated = extended.astype(jnp.float32) + jax.nn.gelu(preact, approximate=False)
        extended = jnp.where(inside[None, :], updated, 0.0).astype(jnp.bfloat16)
    hidden = extended[:, reach : reach + frames]
    portion = lax.all_gather(hidden, "sensor", axis=0, tiled=True)
    key_rows = jnp.dot(key_w, portion, preferred_element_type=jnp.float32)
    value_rows = jnp.dot(value_w, portion, preferred_element_type=jnp.float32)
    head_count = key_w.shape[0] // HD
    key_heads = key_rows.astype(jnp.bfloat16).reshape(head_count, HD, frames)
    value_heads = value_rows.astype(jnp.bfloat16).reshape(head_count, HD, frames)
    frame_mask = jnp.arange(frames, dtype=jnp.int32) < valid_frames[0]
    block_rows = min(LATENTS, 512)
    block_count = LATENTS // block_rows
    query_blocks = queries.reshape(head_count, HD, block_count, block_rows).transpose(2, 0, 1, 3)
    scale = 1.0 / math.sqrt(HD)

    def attend(query_block):
        scores = (
            jnp.einsum("hdq,hdt->hqt", query_block, key_heads, preferred_element_type=jnp.float32)
            * scale
        )
        scores = jnp.where(frame_mask[None, None, :], scores, -jnp.inf)
        peaks = jnp.max(scores, axis=2)
        probs = jnp.where(frame_mask[None, None, :], jnp.exp(scores - peaks[:, :, None]), 0.0)
        totals = jnp.sum(probs, axis=2)
        weighted = jnp.einsum(
            "hqt,hdt->hdq",
            probs.astype(jnp.bfloat16),
            value_heads,
            preferred_element_type=jnp.float32,
        )
        return (peaks, totals, weighted)

    peaks, totals, weighted = lax.map(attend, query_blocks)
    peaks = peaks.transpose(1, 0, 2).reshape(head_count, LATENTS)
    totals = totals.transpose(1, 0, 2).reshape(head_count, LATENTS)
    weighted = weighted.transpose(1, 2, 0, 3).reshape(head_count, HD, LATENTS)
    global_peaks = lax.pmax(peaks, "tm")
    rescale = jnp.exp(peaks - global_peaks)
    totals, weighted = lax.psum((totals * rescale, weighted * rescale[:, None, :]), "tm")
    attended = (
        (weighted / totals[:, None, :]).reshape(head_count * HD, LATENTS).astype(jnp.bfloat16)
    )
    return (hidden, attended)


def solution(mesh):
    return jax.shard_map(
        on_device,
        mesh=mesh,
        in_specs=(
            P("sensor", "tm"),
            P(None, "sensor"),
            P(None, None, "sensor", None),
            P(None, "sensor"),
            P(),
            P("tm"),
            P("sensor", None),
            P("sensor", None),
            P("sensor", None),
        ),
        out_specs=(P("sensor", "tm"), P("sensor", None)),
        check_vma=False,
    )
```

profile of v0, /device:TPU:0, one launch (start us, length us, event | category | flops | bytes accessed | tf_op | source)
XLA Modules:
  0.0 366.2 jit_solution(9976685040315797149)
XLA Ops:
  8.1 2.7 fusion.128
  10.9 34.7 %reduce-scatter.2.cloned.1.call-done = f32[256,1024]{0,1:T(8,128)} async-done(((f32[512,1024]{0,1:T(8,128)}), f32[256,1024]{0,1:T(8,128)}) %reduce-scatter.2.cloned.1.call-update) | async-done | bytes 1048592 | tf_op jit(solution)/shard_map/reduce_scatter | solution.py:49
  45.6 1.4 convert_element_type.46
  47.1 1.6 collective-permute-start
  50.0 3.2 collective-permute-done.1
  56.7 22.1 %all-gather.5.cloned.1.call-done = bf16[512,1120]{0,1:T(8,128)(2,1)} async-done(((bf16[256,1120]{0,1:T(8,128)(2,1)}), bf16[512,1120]{0,1:T(8,128)(2,1)}) %all-gather.5.cloned.1.call-update) | async-done | bytes 1146896 | tf_op jit(solution)/shard_map/all_gather | solution.py:64
  78.8 1.9 fusion.72
  81.2 4.2 %fusion.26 = bf16[256,1120]{0,1:T(8,128)(2,1)} fusion(f32[1120,256]{1,0:T(8,128)S(1)} %fusion.72, f32[1120,256]{1,0:T(8,128)S(1)} %convolution_add_fusion.7, bf16[512,1120]{0,1:T(8,128)(2,1)S(1)} %copy-done.6, pred[1120]{0:T(1024)(128)(4,1)S(1)} %fusion.111, bf16[3,3,256,512]{3,2,1,0:T(8,128)(2,1)S(1)} %copy-done.9, ...), kind=kOutput, calls=%fused_computation.38 | convolution fusion | flops 315105280 | bytes 4851712 | tf_op jit(solution)/shard_map/dot_general | solution.py:38
  87.4 20.5 %all-gather.7.cloned.1.call-done = bf16[512,1120]{0,1:T(8,128)(2,1)} async-done(((bf16[256,1120]{0,1:T(8,128)(2,1)}), bf16[512,1120]{0,1:T(8,128)(2,1)}) %all-gather.7.cloned.1.call-update) | async-done | bytes 1146896 | tf_op jit(solution)/shard_map/all_gather | solution.py:64
  107.9 1.9 convolution_add_fusion.5
  110.9 4.0 %fusion.31 = bf16[256,1120]{0,1:T(8,128)(2,1)} fusion(bf16[256,1120]{0,1:T(8,128)(2,1)S(1)} %copy-done.8, f32[1120,256]{1,0:T(8,128)S(1)} %convolution_add_fusion.4, s32[]{:T(128)S(6)} %select_n.39, bf16[512,1120]{0,1:T(8,128)(2,1)S(1)} %copy-done.5, pred[1120]{0:T(1024)(128)(4,1)S(1)} %fusion.111, bf16[3,3,256,512]{3,2,1,0:T(8,128)(2,1)S(1)} %copy-done.9), kind=kOutput, calls=%fused_computation.43 | convolution fusion | flops 313384960 | bytes 3704836 | tf_op jit(solution)/shard_map/dot_general | solution.py:38
  116.7 20.7 %all-gather.9.cloned.1.call-done = bf16[512,1120]{0,1:T(8,128)(2,1)} async-done(((bf16[256,1120]{0,1:T(8,128)(2,1)}), bf16[512,1120]{0,1:T(8,128)(2,1)}) %all-gather.9.cloned.1.call-update) | async-done | bytes 1146896 | tf_op jit(solution)/shard_map/all_gather | solution.py:64
  137.5 1.9 convolution_add_fusion.2
  139.8 2.6 bitcast_abs_fusion
  146.2 20.1 %all-gather.11.cloned.1.call-done = bf16[512,1024]{0,1:T(8,128)(2,1)} async-done(((bf16[256,1024]{0,1:T(8,128)(2,1)}), bf16[512,1024]{0,1:T(8,128)(2,1)}) %all-gather.11.cloned.1.call-update) | async-done | bytes 1048592 | tf_op jit(solution)/shard_map/all_gather | solution.py:69
  166.3 1.8 convolution_convert_fusion.1
  168.6 28.8 %while.15 = (s32[]{:T(128)}, f32[4,4,512]{2,1,0:T(4,128)S(1)}, f32[4,4,512]{2,1,0:T(4,128)S(1)}, f32[4,4,64,512]{3,2,1,0:T(8,128)}, bf16[4,4,64,512]{3,2,1,0:T(8...) while((s32[]{:T(128)}, f32[4,4,512]{2,1,0:T(4,128)S(1)}, ...), condition=%wide.region_4.5_spmd.clone, body=%wide.region_1.4_spmd.clone.sunk | while | flops 564130816 | bytes 27071080 | solution.py:98
  169.3 1.4 fusion.149
  170.7 2.9 fusion.151
  173.6 2.3 fusion.150
  177.9 2.9 fusion.151
  180.8 2.3 fusion.150
  185.1 2.8 fusion.151
  188.0 2.3 fusion.150
  192.3 2.9 fusion.151
  195.2 2.3 fusion.150
  197.5 61.0 %pmax.7 = f32[4,2048]{1,0:T(4,128)S(1)} all-reduce(f32[4,2048]{1,0:T(4,128)S(1)} %bitcast.276), channel_id=1, replica_groups=mesh['sensor'=2,'tm'=16] {'tm'}, use_global_device_ids=true, to_apply=%region_5.6 | all-reduce | flops 8192 | bytes 65536 | tf_op jit(solution)/shard_map/pmax | solution.py:102
  258.5 1.8 copy.36
  260.3 1.5 broadcast_multiply_fusion
  263.9 58.3 %psum.15 = f32[4,2048]{1,0:T(4,128)S(1)} all-reduce(f32[4,2048]{1,0:T(4,128)S(1)} %get-tuple-element.102), channel_id=1, replica_groups=mesh['sensor'=2,'tm'=16] {'tm'}, use_global_device_ids=true, to_apply=%region_7.8 | all-reduce | flops 8192 | bytes 65536 | tf_op jit(solution)/shard_map/psum | solution.py:104
  322.2 34.4 %all-reduce.5.cloned.1.call-done = f32[4,64,2048]{2,1,0:T(8,128)} async-done(((f32[4,64,2048]{2,1,0:T(8,128)}), f32[4,64,2048]{2,1,0:T(8,128)}) %all-reduce.5.cloned.1.call-update) | async-done | bytes 2097168 | tf_op jit(solution)/shard_map/psum | solution.py:104
  356.6 2.7 divide_convert_fusion
  (73 shorter events, 19.1 us)
Async XLA Ops:
  7.2 1.0 copy-start
  7.2 38.5 %reduce-scatter.2.cloned.1.call-start = ((), (), s32[]{:S(2)}) async-start(), calls=%async_computation.1 | async-start | bytes 3145728 | tf_op jit(solution)/shard_map/reduce_scatter | solution.py:49
  10.9 67.9 %all-gather.5.cloned.1.call-start = ((), (), s32[]{:S(2)}) async-start(), calls=%async_computation.2 | async-start | bytes 1720320 | tf_op jit(solution)/shard_map/all_gather | solution.py:64
  45.6 33.1 %copy-start.9 = (bf16[3,3,256,512]{3,2,1,0:T(8,128)(2,1)S(1)}, bf16[3,3,256,512]{3,2,1,0:T(8,128)(2,1)}, u32[]{:S(2)}) copy-start(bf16[3,3,256,512]{3,2,1,0:T(8,128)(2,1)} %param.13) | copy-start | bytes 7077892
  47.1 7.1 %copy-start.12 = (s32[3]{0:T(128)S(1)}, s32[3]{0:T(128)}, u32[]{:S(2)}) copy-start(s32[3]{0:T(128)} %param.15) | copy-start | bytes 40
  47.1 9.6 %copy-start.13 = (f32[3,256]{1,0:T(4,128)S(1)}, f32[3,256]{1,0:T(4,128)}, u32[]{:S(2)}) copy-start(f32[3,256]{1,0:T(4,128)} %param.14) | copy-start | bytes 9220
  47.1 2.9 collective-permute-start
  48.7 4.5 %collective-permute-start.1 = (bf16[256,48]{0,1:T(8,128)(2,1)S(1)}, bf16[256,48]{0,1:T(8,128)(2,1)S(1)}, u32[]{:S(2)}, u32[]{:S(2)}) collective-permute-start(bf16[256,48]{0,1:T(8,128)(2,1)S(1)} %get-tuple-element.115), channel_id=1, source_target_pairs={{1,0},{2,1},{3,2},{4,3},{5,4},{6,5},{7,6},{8,7},{9,8},{10,9},{11,1... | collective-permute-start | bytes 73736 | tf_op jit(solution)/shard_map/ppermute | solution.py:23
  54.1 53.9 %all-gather.7.cloned.1.call-start = ((), (), s32[]{:S(2)}) async-start(), calls=%async_computation.3 | async-start | bytes 1720320 | tf_op jit(solution)/shard_map/all_gather | solution.py:64
  78.8 1.9 copy-start.6
  85.4 52.0 %all-gather.9.cloned.1.call-start = ((), (), s32[]{:S(2)}) async-start(), calls=%async_computation.4 | async-start | bytes 1720320 | tf_op jit(solution)/shard_map/all_gather | solution.py:64
  107.9 1.9 copy-start.5
  109.8 1.1 copy-start.8
  114.9 51.4 %all-gather.11.cloned.1.call-start = ((), (), s32[]{:S(2)}) async-start(), calls=%async_computation.5 | async-start | bytes 1572864 | tf_op jit(solution)/shard_map/all_gather | solution.py:69
  137.5 1.9 copy-start.4
  142.6 1.1 copy-start.3
  143.6 1.5 copy-start.7
  144.9 211.7 %all-reduce.5.cloned.1.call-start = ((), (), s32[]{:S(2)}) async-start(), calls=%async_computation.6 | async-start | bytes 4194304 | tf_op jit(solution)/shard_map/psum | solution.py:104
  146.0 20.3 %copy-start.10 = (bf16[256,512]{1,0:T(8,128)(2,1)S(1)}, bf16[256,512]{1,0:T(8,128)(2,1)}, u32[]{:S(2)}) copy-start(bf16[256,512]{1,0:T(8,128)(2,1)} %param.17) | copy-start | bytes 786436
  146.2 21.9 %copy-start.11 = (bf16[256,512]{1,0:T(8,128)(2,1)S(1)}, bf16[256,512]{1,0:T(8,128)(2,1)}, u32[]{:S(2)}) copy-start(bf16[256,512]{1,0:T(8,128)(2,1)} %param.18) | copy-start | bytes 786436
  166.3 1.8 copy-start.2
  261.9 1.0 copy-start.1
Sparse Core Ops, SparseCore 0:
  11.0 34.6 reduce-scatter.1
  54.2 24.5 all-gather.4
  85.6 22.3 all-gather.6
  115.1 22.3 all-gather.8
  145.0 21.2 all-gather.10
  262.0 94.5 all-reduce.4
where the time goes:
time: 367 us; the launch traced here: 366 us
  waiting for transfers between devices  156 us (43%)
  blocking collectives  119 us (32%)
  matrix products  40 us (11%)
  between operations  20 us (5%)
  other arithmetic  19.8 us (5%)
  local copies, waits for them, and re-layouts  7.85 us (2%)
    all_gather x3, waiting for transfers between devices, on_device(): lax.all_gather(extended, 'sensor', axis=0, tiled=True)  63.3 us
    pmax x1, blocking collectives, on_device(): global_peaks = lax.pmax(peaks, 'tm')  61 us
    psum x1, blocking collectives, on_device(): lax.psum((totals * rescale, weighted * rescale[:, None, :]), 'tm')  58.3 us
    reduce_scatter x1, waiting for transfers between devices, on_device(): lax.psum_scatter(jnp.dot(spatial_w, recording, preferred_element_type=jnp...  34.7 us
    psum x1, waiting for transfers between devices, on_device(): lax.psum((totals * rescale, weighted * rescale[:, None, :]), 'tm')  34.4 us
    all_gather x1, waiting for transfers between devices, on_device(): portion = lax.all_gather(hidden, 'sensor', axis=0, tiled=True)  20.1 us
    dot_general x9, matrix products, add_taps(): jnp.dot(kernel, shifted, preferred_element_type=jnp.float32)  18 us
    dot_general x4, matrix products, attend(): jnp.einsum('hqt,hdt->hdq', probs.astype(jnp.bfloat16), value_heads, prefe...  11.4 us
  transfers between devices with their start and end apart: 8, of which 7 were waited for; matrix products, arithmetic and copies ran while one was open for 1% of the time, Pallas kernels for 0%

commit v1 on v0

--- a/solution.py
+++ b/solution.py
@@ -8,6 +8,18 @@
 LATENTS = 2048
 LAYERS = 3
 DMAX = 16
+
+
+def doubled_up(shard, axis, dim):
+    ways, here, step = (lax.axis_size(axis), lax.axis_index(axis), shard.shape[dim])
+    line, have = (shard, 1)
+    while have < ways:
+        line = jnp.concatenate(
+            [line, lax.ppermute(line, axis, [(d, (d - have) % ways) for d in range(ways)])],
+            axis=dim,
+        )
+        have = 2 * have
+    return jnp.roll(line, here * step, axis=dim)
 
 
 def padded(cells, sides, width):
@@ -60,9 +72,7 @@
     for layer in range(LAYERS):
         initial = jnp.broadcast_to(conv_b[layer][:, None], (ch_loc, span))
         folder = tap_folder(conv_w[layer], dilations[layer], span, DMAX)
-        preact = folder(
-            initial, lax.all_gather(extended, "sensor", axis=0, tiled=True), jnp.int32(0)
-        )
+        preact = folder(initial, doubled_up(extended, "sensor", 0), jnp.int32(0))
         updated = extended.astype(jnp.float32) + jax.nn.gelu(preact, approximate=False)
         extended = jnp.where(inside[None, :], updated, 0.0).astype(jnp.bfloat16)
     hidden = extended[:, reach : reach + frames]

time: 367 us -> 348 us (0.948)
  waiting for transfers between devices: 156 us -> 129 us
  other arithmetic: 19.8 us -> 23.8 us
    all_gather x3 -> x0, waiting for transfers between devices: 63.3 us -> none  [on_device(): lax.all_gather(extended, 'sensor', axis=0, tiled=True)]
    ppermute x0 -> x3, waiting for transfers between devices: none -> 36.7 us  [doubled_up(): lax.ppermute(line, axis, [(d, (d - have) % ways) for d in range(ways)])]
    concatenate x0 -> x3, other arithmetic: none -> 5 us  [doubled_up(): return jnp.roll(line, here * step, axis=dim)]
where the time goes in v1:
time: 348 us; the launch traced here: 347 us
  waiting for transfers between devices  129 us (37%)
  blocking collectives  119 us (34%)
  matrix products  43.4 us (12%)
  other arithmetic  23.8 us (7%)
  between operations  19.9 us (6%)
  local copies, waits for them, and re-layouts  6.73 us (2%)
  starting transfers between devices  4.8 us (1%)
    pmax x1, blocking collectives, on_device(): global_peaks = lax.pmax(peaks, 'tm')  61 us
    psum x1, blocking collectives, on_device(): lax.psum((totals * rescale, weighted * rescale[:, None, :]), 'tm')  58.4 us
    ppermute x3, waiting for transfers between devices, doubled_up(): lax.ppermute(line, axis, [(d, (d - have) % ways) for d in range(ways)])  36.7 us
    reduce_scatter x1, waiting for transfers between devices, on_device(): lax.psum_scatter(jnp.dot(spatial_w, recording, preferred_element_type=jnp...  34.7 us
    psum x1, waiting for transfers between devices, on_device(): lax.psum((totals * rescale, weighted * rescale[:, None, :]), 'tm')  34.2 us
    dot_general x9, matrix products, add_taps(): jnp.dot(kernel, shifted, preferred_element_type=jnp.float32)  21.3 us
    all_gather x1, waiting for transfers between devices, on_device(): portion = lax.all_gather(hidden, 'sensor', axis=0, tiled=True)  20.3 us
    dot_general x4, matrix products, attend(): jnp.einsum('hqt,hdt->hdq', probs.astype(jnp.bfloat16), value_heads, prefe...  11.4 us
  transfers between devices with their start and end apart: 8, of which 7 were waited for; matrix products, arithmetic and copies ran while one was open for 1% of the time, Pallas kernels for 0%

profile of v1, /device:TPU:0, one launch (start us, length us, event | category | flops | bytes accessed | tf_op | source)
XLA Modules:
  0.0 347.3 jit_solution(6038045827443462995)
XLA Ops:
  8.1 2.7 fusion.141
  10.9 34.7 %reduce-scatter.2.cloned.1.call-done = f32[256,1024]{0,1:T(8,128)} async-done(((f32[512,1024]{0,1:T(8,128)}), f32[256,1024]{0,1:T(8,128)}) %reduce-scatter.2.cloned.1.call-update) | async-done | bytes 1048592 | tf_op jit(solution)/shard_map/reduce_scatter | solution.py:61
  46.9 1.6 collective-permute-start
  49.8 3.2 collective-permute-done.1
  56.3 11.1 %collective-permute-done.2 = bf16[256,1120]{0,1:T(8,128)(2,1)S(1)} collective-permute-done((bf16[256,1120]{0,1:T(8,128)(2,1)S(1)}, bf16[256,1120]{0,1:T(8,128)(2,1)S(1)}, u32[]{:S(2)}, u32[]{:S(2)}) %collective-permute-start.2) | collective-permute-done | bytes 573472 | tf_op jit(solution)/shard_map/ppermute | solution.py:18
  67.4 3.5 %fusion.40 = bf16[512,1120]{0,1:T(8,128)(2,1)S(1)} fusion(s32[]{:T(128)S(6)} %select_n.61, bf16[256,48]{0,1:T(8,128)(2,1)S(1)} %collective-permute-done, bf16[256,1024]{0,1:T(8,128)(2,1)S(1)} %convert_element_type.46, bf16[256,48]{0,1:T(8,128)(2,1)S(1)} %collective-permute-done.1, bf16[256,1120]{0,1:T(8,128)(2,1)S(1)} %collective-permute-done.2), kind=kLoop, calls=%fused_computation.69 | loop fusion | flops 9175040 | bytes 2293764 | tf_op jit(solution)/shard_map/jit(_roll_dynamic)/concatenate | solution.py:22
  70.9 1.5 convolution_add_fusion.8
  72.4 1.5 convolution_add_fusion.7
  73.9 4.7 %fusion.25 = bf16[256,1120]{0,1:T(8,128)(2,1)S(1)} fusion(f32[1120,256]{1,0:T(8,128)S(1)} %convolution_add_fusion.7, s32[]{:T(128)S(6)} %select_n.46, bf16[512,1120]{0,1:T(8,128)(2,1)S(1)} %fusion.40, pred[1120]{0:T(1024)(128)(4,1)S(1)} %fusion.124, bf16[3,3,256,512]{3,2,1,0:T(8,128)(2,1)} %param.15, bf16[256,48]{0,1:T(8,128)(2,1)S(1)} %collective-permute-done.1, ...), kind=kOutput, calls=%fused_computation.54 | convolution fusion | flops 314818560 | bytes 3703908 | tf_op jit(solution)/shard_map/dot_general | solution.py:50
  81.1 12.9 %collective-permute-done.3 = bf16[256,1120]{0,1:T(8,128)(2,1)S(1)} collective-permute-done((bf16[256,1120]{0,1:T(8,128)(2,1)S(1)}, bf16[256,1120]{0,1:T(8,128)(2,1)S(1)}, u32[]{:S(2)}, u32[]{:S(2)}) %collective-permute-start.3) | collective-permute-done | bytes 573472 | tf_op jit(solution)/shard_map/ppermute | solution.py:18
  94.8 1.5 convolution_add_fusion.5
  97.7 4.3 %fusion.30 = bf16[256,1120]{0,1:T(8,128)(2,1)S(1)} fusion(bf16[256,1120]{0,1:T(8,128)(2,1)S(1)} %fusion.25, f32[1120,256]{1,0:T(8,128)S(1)} %convolution_add_fusion.4, s32[]{:T(128)S(6)} %select_n.49, bf16[512,1120]{0,1:T(8,128)(2,1)S(1)} %fusion.35, pred[1120]{0:T(1024)(128)(4,1)S(1)} %fusion.124, bf16[3,3,256,512]{3,2,1,0:T(8,128)(2,1)} %param.15), kind=kOutput, calls=%fused_computation.59 | convolution fusion | flops 313384960 | bytes 3703908 | tf_op jit(solution)/shard_map/dot_general | solution.py:50
  104.6 12.6 %collective-permute-done.4 = bf16[256,1120]{0,1:T(8,128)(2,1)S(1)} collective-permute-done((bf16[256,1120]{0,1:T(8,128)(2,1)S(1)}, bf16[256,1120]{0,1:T(8,128)(2,1)S(1)}, u32[]{:S(2)}, u32[]{:S(2)}) %collective-permute-start.4) | collective-permute-done | bytes 573472 | tf_op jit(solution)/shard_map/ppermute | solution.py:18
  118.0 1.5 convolution_add_fusion.2
  120.9 3.6 %bitcast_abs_fusion = (f32[256,1120]{0,1:T(8,128)S(1)}, f32[256,1120]{0,1:T(8,128)S(1)}, f32[256,1120]{0,1:T(8,128)S(1)}, f32[256,1120]{0,1:T(8,128)S(1)}, f32[1120,256]{1,0:T(8,128)S(1)}) fusion(f32[1120,256]{1,0:T(8,128)S(1)} %convolution_add_fusion.1, bf16[3,3,256,512]{3,2,1,0:T(8,128)(2,1)} %param.15, s32[]{:T(128)S(6)} %select_n.52, ...), kind=kOutput, calls=%fused_computation.76 | convolution fusion | flops 310231040 | bytes 8290308 | tf_op jit(solution)/shard_map/dot_general | solution.py:50
  127.4 20.3 %all-gather.2.cloned.1.call-done = bf16[512,1024]{0,1:T(8,128)(2,1)} async-done(((bf16[256,1024]{0,1:T(8,128)(2,1)}), bf16[512,1024]{0,1:T(8,128)(2,1)}) %all-gather.2.cloned.1.call-update) | async-done | bytes 1048592 | tf_op jit(solution)/shard_map/all_gather | solution.py:79
  147.8 1.8 convolution_convert_fusion.1
  150.1 28.9 %while.15 = (s32[]{:T(128)}, f32[4,4,512]{2,1,0:T(4,128)S(1)}, f32[4,4,512]{2,1,0:T(4,128)S(1)}, f32[4,4,64,512]{3,2,1,0:T(8,128)}, bf16[4,4,64,512]{3,2,1,0:T(8...) while((s32[]{:T(128)}, f32[4,4,512]{2,1,0:T(4,128)S(1)}, ...), condition=%wide.region_4.6_spmd.clone, body=%wide.region_1.5_spmd.clone.sunk | while | flops 564130816 | bytes 27071080 | solution.py:108
  152.2 2.9 fusion.164
  155.0 2.3 fusion.163
  159.4 2.9 fusion.164
  162.2 2.3 fusion.163
  166.6 2.8 fusion.164
  169.4 2.3 fusion.163
  173.8 2.9 fusion.164
  176.7 2.3 fusion.163
  179.0 61.0 %pmax.7 = f32[4,2048]{1,0:T(4,128)S(1)} all-reduce(f32[4,2048]{1,0:T(4,128)S(1)} %bitcast.276), channel_id=1, replica_groups=mesh['sensor'=2,'tm'=16] {'tm'}, use_global_device_ids=true, to_apply=%region_5.7 | all-reduce | flops 8192 | bytes 65536 | tf_op jit(solution)/shard_map/pmax | solution.py:112
  240.0 1.8 copy.53
  241.8 1.5 broadcast_multiply_fusion
  245.4 58.4 %psum.15 = f32[4,2048]{1,0:T(4,128)S(1)} all-reduce(f32[4,2048]{1,0:T(4,128)S(1)} %get-tuple-element.111), channel_id=1, replica_groups=mesh['sensor'=2,'tm'=16] {'tm'}, use_global_device_ids=true, to_apply=%region_7.9 | all-reduce | flops 8192 | bytes 65536 | tf_op jit(solution)/shard_map/psum | solution.py:114
  303.8 34.2 %all-reduce.5.cloned.1.call-done = f32[4,64,2048]{2,1,0:T(8,128)} async-done(((f32[4,64,2048]{2,1,0:T(8,128)}), f32[4,64,2048]{2,1,0:T(8,128)}) %all-reduce.5.cloned.1.call-update) | async-done | bytes 2097168 | tf_op jit(solution)/shard_map/psum | solution.py:114
  338.1 2.7 divide_convert_fusion
  (61 shorter events, 24.2 us)
Async XLA Ops:
  7.2 1.0 copy-start
  7.2 38.5 %reduce-scatter.2.cloned.1.call-start = ((), (), s32[]{:S(2)}) async-start(), calls=%async_computation.1 | async-start | bytes 3145728 | tf_op jit(solution)/shard_map/reduce_scatter | solution.py:61
  10.9 42.8 %copy-start.6 = (s32[3]{0:T(128)S(1)}, s32[3]{0:T(128)}, u32[]{:S(2)}) copy-start(s32[3]{0:T(128)} %param.17) | copy-start | bytes 40
  10.9 45.4 %copy-start.7 = (f32[3,256]{1,0:T(4,128)S(1)}, f32[3,256]{1,0:T(4,128)}, u32[]{:S(2)}) copy-start(f32[3,256]{1,0:T(4,128)} %param.16) | copy-start | bytes 9220
  10.9 136.9 %all-gather.2.cloned.1.call-start = ((), (), s32[]{:S(2)}) async-start(), calls=%async_computation.2 | async-start | bytes 1572864 | tf_op jit(solution)/shard_map/all_gather | solution.py:79
  46.9 2.9 collective-permute-start
  48.5 4.5 %collective-permute-start.1 = (bf16[256,48]{0,1:T(8,128)(2,1)S(1)}, bf16[256,48]{0,1:T(8,128)(2,1)S(1)}, u32[]{:S(2)}, u32[]{:S(2)}) collective-permute-start(bf16[256,48]{0,1:T(8,128)(2,1)S(1)} %get-tuple-element.123), channel_id=1, source_target_pairs={{1,0},{2,1},{3,2},{4,3},{5,4},{6,5},{7,6},{8,7},{9,8},{10,9},{11,1... | collective-permute-start | bytes 73736 | tf_op jit(solution)/shard_map/ppermute | solution.py:35
  53.1 14.3 %collective-permute-start.2 = (bf16[256,1120]{0,1:T(8,128)(2,1)S(1)}, bf16[256,1120]{0,1:T(8,128)(2,1)S(1)}, u32[]{:S(2)}, u32[]{:S(2)}) collective-permute-start(bf16[256,1120]{0,1:T(8,128)(2,1)S(1)} %pad_maximum_fusion), channel_id=1, source_target_pairs={{0,16},{16,0},{1,17},{17,1},{2,18},{18,2},{3,19},{19,3},{4,20},{20... | collective-permute-start | bytes 1720328 | tf_op jit(solution)/shard_map/ppermute | solution.py:18
  78.5 15.5 %collective-permute-start.3 = (bf16[256,1120]{0,1:T(8,128)(2,1)S(1)}, bf16[256,1120]{0,1:T(8,128)(2,1)S(1)}, u32[]{:S(2)}, u32[]{:S(2)}) collective-permute-start(bf16[256,1120]{0,1:T(8,128)(2,1)S(1)} %fusion.25), channel_id=1, source_target_pairs={{0,16},{16,0},{1,17},{17,1},{2,18},{18,2},{3,19},{19,3},{4,20},{20... | collective-permute-start | bytes 1720328 | tf_op jit(solution)/shard_map/ppermute | solution.py:18
  102.0 15.2 %collective-permute-start.4 = (bf16[256,1120]{0,1:T(8,128)(2,1)S(1)}, bf16[256,1120]{0,1:T(8,128)(2,1)S(1)}, u32[]{:S(2)}, u32[]{:S(2)}) collective-permute-start(bf16[256,1120]{0,1:T(8,128)(2,1)S(1)} %fusion.30), channel_id=1, source_target_pairs={{0,16},{16,0},{1,17},{17,1},{2,18},{18,2},{3,19},{19,3},{4,20},{20... | collective-permute-start | bytes 1720328 | tf_op jit(solution)/shard_map/ppermute | solution.py:18
  124.8 1.4 copy-start.3
  126.1 212.0 %all-reduce.5.cloned.1.call-start = ((), (), s32[]{:S(2)}) async-start(), calls=%async_computation.3 | async-start | bytes 4194304 | tf_op jit(solution)/shard_map/psum | solution.py:114
  127.2 20.6 %copy-start.4 = (bf16[256,512]{1,0:T(8,128)(2,1)S(1)}, bf16[256,512]{1,0:T(8,128)(2,1)}, u32[]{:S(2)}) copy-start(bf16[256,512]{1,0:T(8,128)(2,1)} %param.19) | copy-start | bytes 786436
  127.4 22.1 %copy-start.5 = (bf16[256,512]{1,0:T(8,128)(2,1)S(1)}, bf16[256,512]{1,0:T(8,128)(2,1)}, u32[]{:S(2)}) copy-start(bf16[256,512]{1,0:T(8,128)(2,1)} %param.20) | copy-start | bytes 786436
  147.8 1.8 copy-start.2
  243.4 1.0 copy-start.1
Sparse Core Ops, SparseCore 0:
  11.0 34.6 reduce-scatter.1
  126.2 21.5 all-gather.1
  243.5 94.4 all-reduce.4
